TPU v7x, 32 devices: a whole 2x2x4 slice. The times are simulated.
32 devices in a mesh: tower: 4 (over y, x), rank: 8 (over z, core).
Axes of the slice: x: 2, y: 2, z: 4, core: 2. Of those that a mesh axis runs over, the one named last changes fastest.
Arguments:
- pooled: bfloat16 [2, 2048, 1024], P(None, ('tower', 'rank')), may hold values from -8 to 8
- feature_order: int32 [4, 4], P('tower'), may hold values from 0 to 3, as said below
- cross_weight: bfloat16 [4, 3, 512, 512], P('tower'), may hold values from -0.25 to 0.25
- cross_bias: float32 [4, 3, 512], P('tower'), may hold values from -3 to 3
- compress_weight: bfloat16 [4, 128, 512], P('tower'), may hold values from -0.25 to 0.25
- norm_gain: float32 [4, 128], P('tower'), may hold values from 0.1 to 1.9
- mlp_weight: bfloat16 [4096, 512], P(('tower', 'rank')), may hold values from -0.25 to 0.25
- mlp_bias: bfloat16 [4096], P(('tower', 'rank')), may hold values from -3 to 3
- out_weight: bfloat16 [4096], P(('tower', 'rank')), may hold values from -0.09375 to 0.09375
Outputs:
- logits: float32 [2, 8, 128], P(None, 'rank', 'tower')
Inputs may be any that keep to these rules, and one draw needn't show every extreme that they name: `feature_order`: each row is an ordering of 0 to 3.
All inputs are finite; a program needn't handle non-finite values.
Results may differ from a plain program's by a relative error of at most 0.0076.
Values may be sent and summed in bfloat16 or wider, within the bound.
A program may use at most 64 MiB of HBM per device.

v0:
```python
import jax
import jax.numpy as jnp
from jax import lax
from jax.sharding import PartitionSpec as P

E = 128
CD = 128
epsilon = 1e-06


def tower_block(first, weights, biases, compress, gain):
    first_f = first.astype(jnp.float32)
    current = first
    for layer in range(weights.shape[0]):
        product = (
            jnp.dot(weights[layer], current, preferred_element_type=jnp.float32)
            + biases[layer][:, None]
        )
        current = (first_f * product + current.astype(jnp.float32)).astype(jnp.bfloat16)
    squeezed = jnp.dot(compress, current, preferred_element_type=jnp.float32)
    inverse_rms = lax.rsqrt(jnp.mean(squeezed * squeezed, axis=0, keepdims=True) + epsilon)
    return (squeezed * inverse_rms * gain[:, None]).astype(jnp.bfloat16)


def interact(joined):
    samples_now = joined.shape[1]
    values_f = joined.astype(jnp.float32).reshape(-1, CD, samples_now)
    gram = jnp.einsum("tck,uck->tuk", values_f, values_f, precision=lax.Precision.HIGHEST) / CD
    mixed = values_f + jnp.einsum("tuk,uck->tck", gram, values_f, precision=lax.Precision.HIGHEST)
    return mixed.reshape(-1, samples_now).astype(jnp.bfloat16)


def logit_terms(hidden_rows, hidden_bias, hidden_out, features):
    hidden = (
        jnp.dot(hidden_rows, features, preferred_element_type=jnp.float32)
        + hidden_bias.astype(jnp.float32)[:, None]
    )
    return jnp.sum(
        jax.nn.relu(hidden) * hidden_out.astype(jnp.float32)[:, None], axis=0, keepdims=True
    )


def on_device(
    pooled,
    feature_order,
    cross_weight,
    cross_bias,
    compress_weight,
    norm_gain,
    mlp_weight,
    mlp_bias,
    out_weight,
):
    micro_count = pooled.shape[0]
    arriving = [
        lax.all_to_all(pooled[batch], "rank", split_axis=1, concat_axis=0, tiled=True)
        for batch in range(micro_count)
    ]
    hidden_rows, hidden_bias, hidden_out = (
        lax.all_gather(mlp_weight, "rank", axis=0, tiled=True),
        lax.all_gather(mlp_bias, "rank", axis=0, tiled=True),
        lax.all_gather(out_weight, "rank", axis=0, tiled=True),
    )
    results = []
    for batch in range(micro_count):
        arrived = arriving[batch]
        samples_here = arrived.shape[1]
        first = jnp.take(arrived.reshape(-1, E, samples_here), feature_order[0], axis=0).reshape(
            -1, samples_here
        )
        compressed = tower_block(
            first, cross_weight[0], cross_bias[0], compress_weight[0], norm_gain[0]
        )
        all_towers = lax.all_gather(compressed, "tower", axis=0, tiled=True)
        partial_value = logit_terms(hidden_rows, hidden_bias, hidden_out, interact(all_towers))
        logit_row = lax.psum_scatter(partial_value, "tower", scatter_dimension=1, tiled=True)
        results.append(logit_row)
    return jnp.stack(results)


def solution(mesh):
    return jax.shard_map(
        on_device,
        mesh=mesh,
        in_specs=(
            P(None, ("tower", "rank"), None),
            P("tower", None),
            P("tower", None, None, None),
            P("tower", None, None),
            P("tower", None, None),
            P("tower", None),
            P(("tower", "rank"), None),
            P(("tower", "rank")),
            P(("tower", "rank")),
        ),
        out_specs=P(None, "rank", "tower"),
        check_vma=False,
    )
```

profile of v0, /device:TPU:0, one launch (start us, length us, event | category | flops | bytes accessed | tf_op | source)
XLA Modules:
  0.0 129.5 jit_solution(2807232870646016834)
XLA Ops:
  6.5 0.0 copy-start
  6.5 0.0 copy-start.7
  6.5 0.0 copy-start.3
  6.5 0.0 copy-start.4
  6.5 0.0 copy-start.1
  6.5 1.0 slice_bitcast_fusion.1
  7.6 0.0 copy-start.5
  7.6 0.7 copy.34
  8.3 6.4 %all-to-all-start = ((bf16[64,8,128]{2,0,1:T(8,128)(2,1)}), bf16[64,8,128]{2,0,1:T(8,128)(2,1)S(1)}, u32[]{:S(2)}, u32[]{:S(2)}) async-start(bf16[64,8,128]{2,0,1:T(8,128)(2,1)} %copy.34), calls=%async_computation | async-start | bytes 262144 | tf_op jit(solution)/shard_map/all_to_all | solution.py:56
  14.6 0.0 all-gather.4.cloned.1.call-start
  14.7 0.7 all-gather.4.cloned.1.call-update
  15.4 0.7 compare_select_fusion
  16.1 0.7 copy.41
  16.8 0.0 copy-done.7
  16.8 4.6 %all-to-all-done = bf16[64,8,128]{2,0,1:T(8,128)(2,1)S(1)} async-done(((bf16[64,8,128]{2,0,1:T(8,128)(2,1)}), bf16[64,8,128]{2,0,1:T(8,128)(2,1)S(1)}, u32[]{:S(2)}, u32[]{:S(2)}) %all-to-all-start) | async-done | bytes 131104 | tf_op jit(solution)/shard_map/all_to_all | solution.py:56
  21.4 3.4 %all-to-all-start.1 = ((bf16[64,8,128]{2,0,1:T(8,128)(2,1)}), bf16[64,8,128]{2,0,1:T(8,128)(2,1)S(1)}, u32[]{:S(2)}, u32[]{:S(2)}) async-start(bf16[64,8,128]{2,0,1:T(8,128)(2,1)} %copy.41), calls=%async_computation.1 | async-start | bytes 262144 | tf_op jit(solution)/shard_map/all_to_all | solution.py:56
  24.8 0.0 reduce-scatter.7.cloned.1.call-start
  24.8 0.0 copy-done.3
  24.8 12.2 %all-gather = bf16[8,1,128]{2,1,0:T(2,128)(2,1)S(1)} all-gather(bf16[1,1,128]{2,1,0:T(2,128)(2,1)S(1)} %bitcast.203), channel_id=1, replica_groups=mesh['tower'=4,'rank'=8] {'rank'}, dimensions={0}, use_global_device_ids=true | all-gather | bytes 2304 | tf_op jit(solution)/shard_map/all_gather | solution.py:61
  37.1 0.0 copy-done.4
  37.1 10.3 %all-gather.1 = bf16[8,1,128]{2,1,0:T(2,128)(2,1)S(1)} all-gather(bf16[1,1,128]{2,1,0:T(2,128)(2,1)S(1)} %bitcast.204), channel_id=1, replica_groups=mesh['tower'=4,'rank'=8] {'rank'}, dimensions={0}, use_global_device_ids=true | all-gather | bytes 2304 | tf_op jit(solution)/shard_map/all_gather | solution.py:62
  47.4 0.0 copy-done.1
  47.4 0.6 gather_fusion
  48.0 0.0 all-to-all-done.1
  48.0 0.6 gather_fusion.1
  48.6 0.1 broadcast_select_fusion.1
  48.7 0.1 copy.51
  48.8 0.1 copy.50
  49.0 0.0 copy-done.5
  49.0 0.3 fusion.30
  49.3 0.3 fusion.31
  49.6 0.3 fusion.34
  49.9 0.0 copy-done
  50.0 0.0 copy-start.2
  50.0 0.5 multiply_reduce_fusion
  50.5 0.3 fusion.32
  50.8 0.5 multiply_reduce_fusion.1
  51.3 0.0 copy-done.2
  51.3 0.1 fusion.66
  51.4 8.5 %all_gather.15 = bf16[512,128]{1,0:T(8,128)(2,1)S(1)} all-gather(bf16[128,128]{1,0:T(8,128)(2,1)S(1)} %get-tuple-element.11), channel_id=1, replica_groups=mesh['tower'=4,'rank'=8] {'tower'}, dimensions={0}, use_global_device_ids=true | all-gather | bytes 163840 | tf_op jit(solution)/shard_map/all_gather | solution.py:74
  59.9 0.1 copy.36
  60.0 8.5 %all_gather.19 = bf16[512,128]{1,0:T(8,128)(2,1)S(1)} all-gather(bf16[128,128]{1,0:T(8,128)(2,1)S(1)} %get-tuple-element.12), channel_id=1, replica_groups=mesh['tower'=4,'rank'=8] {'tower'}, dimensions={0}, use_global_device_ids=true | all-gather | bytes 163840 | tf_op jit(solution)/shard_map/all_gather | solution.py:74
  68.5 0.1 copy.43
  68.6 0.3 fusion.12
  68.9 0.3 fusion.7
  69.2 0.7 fusion.28
  69.9 0.7 fusion.29
  70.6 0.0 all-gather.4.cloned.1.call-done
  70.6 0.0 copy-start.6
  70.6 1.9 %fusion.5 = f32[128]{0:T(128)S(1)} fusion(bf16[1024,512]{1,0:T(8,128)(2,1)} %all-gather.4.cloned.1.call-done, f32[1024]{0:T(1024)S(1)} %bitcast.190, f32[1024]{0:T(1024)S(1)} %bitcast.188, bf16[16,8,4,128]{3,2,1,0:T(4,128)(2,1)S(1)} %bitcast.185), kind=kOutput, calls=%fused_computation.9 | convolution fusion | flops 134741888 | bytes 1188352 | tf_op jit(solution)/shard_map/dot_general | solution.py:35
  72.5 0.8 copy.52
  73.2 0.0 reduce-scatter.7.cloned.1.call-update
  73.3 0.0 reduce-scatter.9.cloned.1.call-start
  73.3 0.0 copy-done.6
  73.3 0.6 fusion.4
  73.9 0.7 copy.54
  74.6 0.0 reduce-scatter.9.cloned.1.call-update
  74.7 20.1 %reduce-scatter.7.cloned.1.call-done = f32[32,1]{1,0:T(8,128)} async-done(((f32[128,1]{1,0:T(8,128)}), f32[32,1]{1,0:T(8,128)}) %reduce-scatter.7.cloned.1.call-update) | async-done | bytes 144
  94.7 0.8 copy.53
  95.5 26.0 %reduce-scatter.9.cloned.1.call-done = f32[32,1]{1,0:T(8,128)} async-done(((f32[128,1]{1,0:T(8,128)}), f32[32,1]{1,0:T(8,128)}) %reduce-scatter.9.cloned.1.call-update) | async-done | bytes 144
  121.6 0.8 copy.55
  122.4 0.6 pad_maximum_fusion
  (8 shorter events, 0.1 us)
Async XLA Ops:
  6.5 43.4 %copy-start = (bf16[1,128,512]{2,1,0:T(8,128)(2,1)S(1)}, bf16[1,128,512]{2,1,0:T(8,128)(2,1)}, u32[]{:S(2)}) copy-start(bf16[1,128,512]{2,1,0:T(8,128)(2,1)} %param.15) | copy-start | bytes 393220
  6.5 10.2 %copy-start.7 = (s32[1,4]{1,0:T(1,128)S(1)}, s32[1,4]{1,0:T(1,128)}, u32[]{:S(2)}) copy-start(s32[1,4]{1,0:T(1,128)} %param.12) | copy-start | bytes 52
  6.5 18.3 %copy-start.3 = (bf16[128]{0:T(256)(128)(2,1)S(1)}, bf16[128]{0:T(256)(128)(2,1)}, u32[]{:S(2)}) copy-start(bf16[128]{0:T(256)(128)(2,1)} %param.18) | copy-start | bytes 772
  6.5 30.5 %copy-start.4 = (bf16[128]{0:T(256)(128)(2,1)S(1)}, bf16[128]{0:T(256)(128)(2,1)}, u32[]{:S(2)}) copy-start(bf16[128]{0:T(256)(128)(2,1)} %param.19) | copy-start | bytes 772
  6.5 40.9 %copy-start.1 = (f32[1,3,512]{2,0,1:T(1,128)S(1)}, f32[1,3,512]{2,0,1:T(1,128)}, u32[]{:S(2)}) copy-start(f32[1,3,512]{2,0,1:T(1,128)} %param.14) | copy-start | bytes 18436
  7.6 41.4 %copy-start.5 = (bf16[1,3,512,512]{3,2,1,0:T(8,128)(2,1)S(1)}, bf16[1,3,512,512]{3,2,1,0:T(8,128)(2,1)}, u32[]{:S(2)}) copy-start(bf16[1,3,512,512]{3,2,1,0:T(8,128)(2,1)} %param.13) | copy-start | bytes 4718596
  8.3 13.1 %all-to-all-start = ((bf16[64,8,128]{2,0,1:T(8,128)(2,1)}), bf16[64,8,128]{2,0,1:T(8,128)(2,1)S(1)}, u32[]{:S(2)}, u32[]{:S(2)}) async-start(bf16[64,8,128]{2,0,1:T(8,128)(2,1)} %copy.34), calls=%async_computation | async-start | bytes 262144 | tf_op jit(solution)/shard_map/all_to_all | solution.py:56
  14.6 56.0 %all-gather.4.cloned.1.call-start = ((), (), s32[]{:S(2)}) async-start(), calls=%async_computation.4 | async-start | bytes 1179648 | tf_op jit(solution)/shard_map/all_gather | solution.py:60
  21.4 26.6 %all-to-all-start.1 = ((bf16[64,8,128]{2,0,1:T(8,128)(2,1)}), bf16[64,8,128]{2,0,1:T(8,128)(2,1)S(1)}, u32[]{:S(2)}, u32[]{:S(2)}) async-start(bf16[64,8,128]{2,0,1:T(8,128)(2,1)} %copy.41), calls=%async_computation.1 | async-start | bytes 262144 | tf_op jit(solution)/shard_map/all_to_all | solution.py:56
  24.8 70.0 %reduce-scatter.7.cloned.1.call-start = ((), (), s32[]{:S(2)}) async-start(), calls=%async_computation.5 | async-start | bytes 81920
  50.0 1.3 %copy-start.2 = (f32[1,128]{1,0:T(1,128)S(1)}, f32[1,128]{1,0:T(1,128)}, u32[]{:S(2)}) copy-start(f32[1,128]{1,0:T(1,128)} %param.16) | copy-start | bytes 1540
  70.6 2.7 %copy-start.6 = (bf16[1024,512]{1,0:T(8,128)(2,1)S(1)}, bf16[1024,512]{1,0:T(8,128)(2,1)}, u32[]{:S(2)}) copy-start(bf16[1024,512]{1,0:T(8,128)(2,1)} %all-gather.4.cloned.1.call-done) | copy-start | bytes 3145732
  73.3 48.3 %reduce-scatter.9.cloned.1.call-start = ((), (), s32[]{:S(2)}) async-start(), calls=%async_computation.6 | async-start | bytes 81920
Sparse Core Ops, SparseCore 0:
  17.1 25.6 all-gather.3
  73.4 21.3 reduce-scatter.6
  97.5 24.0 reduce-scatter.8
where the time goes:
time: 130 us; the launch traced here: 129 us
  waiting for transfers between devices  51.5 us (40%)
  blocking collectives  39.5 us (30%)
  between operations  13.4 us (10%)
  starting transfers between devices  9.84 us (8%)
  local copies, waits for them, and re-layouts  7.22 us (6%)
  matrix products  6.64 us (5%)
  other arithmetic  1.44 us (1%)
    unnamed x5, waiting for transfers between devices  46.8 us
    all_gather x2, blocking collectives, on_device(): all_towers = lax.all_gather(compressed, 'tower', axis=0, tiled=True)  16.9 us
    all_gather x1, blocking collectives, on_device(): lax.all_gather(mlp_bias, 'rank', axis=0, tiled=True)  12.2 us
    all_gather x1, blocking collectives, on_device(): lax.all_gather(out_weight, 'rank', axis=0, tiled=True)  10.3 us
    all_to_all x2, starting transfers between devices, on_device(): lax.all_to_all(pooled[batch], 'rank', split_axis=1, concat_axis=0, tiled=...  9.72 us
    all_to_all x2, waiting for transfers between devices, on_device(): lax.all_to_all(pooled[batch], 'rank', split_axis=1, concat_axis=0, tiled=...  4.63 us
    unnamed x23, local copies, waits for them, and re-layouts  4.19 us
  transfers between devices with their start and end apart: 5, of which 3 were waited for; matrix products, arithmetic and copies ran while one was open for 7% of the time, Pallas kernels for 0%

commit v1 on v0

--- a/solution.py
+++ b/solution.py
@@ -53,7 +53,12 @@
 ):
     micro_count = pooled.shape[0]
     arriving = [
-        lax.all_to_all(pooled[batch], "rank", split_axis=1, concat_axis=0, tiled=True)
+        jnp.concatenate(
+            lax.all_to_all(
+                jnp.stack(jnp.split(pooled[batch], lax.axis_size("rank"), axis=1)), "rank", 0, 0
+            ),
+            axis=0,
+        )
         for batch in range(micro_count)
     ]
     hidden_rows, hidden_bias, hidden_out = (

time: 130 us -> 137 us (1.054)
  local copies, waits for them, and re-layouts: 7.22 us -> 15.5 us
  waiting for transfers between devices: 51.5 us -> 46.9 us
  starting transfers between devices: 9.84 us -> 11.6 us
    unnamed x23 -> x32, local copies, waits for them, and re-layouts: 4.19 us -> 11.6 us
    all_to_all x2, waiting for transfers between devices: 4.63 us -> 0.01 us  [on_device(): lax.all_to_all(jnp.stack(jnp.split(pooled[batch], lax.axis_size('rank'),...]
    all_to_all x2, starting transfers between devices: 9.72 us -> 11.4 us  [on_device(): lax.all_to_all(jnp.stack(jnp.split(pooled[batch], lax.axis_size('rank'),...]
  transfers between devices with their start and end apart: 5 -> 5, of which waited for: 3 -> 2; matrix products, arithmetic and copies ran while one was open for 7% -> 11% of each run, Pallas kernels for 0% -> 0%
where the time goes in v1:
time: 137 us; the launch traced here: 136 us
  waiting for transfers between devices  46.9 us (34%)
  blocking collectives  40.2 us (29%)
  local copies, waits for them, and re-layouts  15.5 us (11%)
  between operations  13.3 us (10%)
  starting transfers between devices  11.6 us (8%)
  matrix products  6.64 us (5%)
  other arithmetic  2.1 us (2%)
    unnamed x5, waiting for transfers between devices  46.9 us
    all_gather x2, blocking collectives, on_device(): all_towers = lax.all_gather(compressed, 'tower', axis=0, tiled=True)  17 us
    all_gather x1, blocking collectives, on_device(): lax.all_gather(mlp_bias, 'rank', axis=0, tiled=True)  12.3 us
    unnamed x32, local copies, waits for them, and re-layouts  11.6 us
    all_to_all x2, starting transfers between devices, on_device(): lax.all_to_all(jnp.stack(jnp.split(pooled[batch], lax.axis_size('rank'),...  11.4 us
    all_gather x1, blocking collectives, on_device(): lax.all_gather(out_weight, 'rank', axis=0, tiled=True)  10.9 us
  transfers between devices with their start and end apart: 5, of which 2 were waited for; matrix products, arithmetic and copies ran while one was open for 11% of the time, Pallas kernels for 0%

profile of v1, /device:TPU:0, one launch (start us, length us, event | category | flops | bytes accessed | tf_op | source)
XLA Modules:
  0.0 136.3 jit_solution(3290781845319269937)
XLA Ops:
  6.5 1.1 slice_bitcast_fusion.1
  7.7 0.6 constant_dynamic-update-slice_fusion.15
  8.3 0.6 constant_dynamic-update-slice_fusion.14
  8.9 0.6 constant_dynamic-update-slice_fusion.13
  9.5 0.6 constant_dynamic-update-slice_fusion.12
  10.1 0.6 constant_dynamic-update-slice_fusion.11
  10.7 0.6 constant_dynamic-update-slice_fusion.10
  11.3 0.6 constant_dynamic-update-slice_fusion.9
  11.9 0.6 constant_dynamic-update-slice_fusion.8
  12.5 6.4 %all-to-all-start.1 = ((bf16[8,64,128]{2,1,0:T(8,128)(2,1)}), bf16[8,64,128]{2,1,0:T(8,128)(2,1)S(1)}, u32[]{:S(2)}, u32[]{:S(2)}) async-start(bf16[8,64,128]{2,1,0:T(8,128)(2,1)} %constant_dynamic-update-slice_fusion.8), calls=%async_computation.1 | async-start | bytes 262144 | tf_op jit(solution)/shard_map/all_to_all | solution.py:57
  18.9 0.0 all-gather.4.cloned.1.call-start
  18.9 0.7 all-gather.4.cloned.1.call-update
  19.6 0.7 compare_select_fusion
  20.2 0.6 constant_dynamic-update-slice_fusion.7
  20.8 0.6 constant_dynamic-update-slice_fusion.6
  21.5 0.6 constant_dynamic-update-slice_fusion.5
  22.1 0.6 constant_dynamic-update-slice_fusion.4
  22.7 0.6 constant_dynamic-update-slice_fusion.3
  23.3 0.6 constant_dynamic-update-slice_fusion.2
  23.9 0.6 constant_dynamic-update-slice_fusion.1
  24.5 0.7 compare_and_fusion
  25.2 0.6 constant_dynamic-update-slice_fusion
  25.8 0.0 all-to-all-done.1
  25.8 5.1 %all-to-all-start = ((bf16[8,64,128]{2,1,0:T(8,128)(2,1)}), bf16[8,64,128]{2,1,0:T(8,128)(2,1)S(1)}, u32[]{:S(2)}, u32[]{:S(2)}) async-start(bf16[8,64,128]{2,1,0:T(8,128)(2,1)} %constant_dynamic-update-slice_fusion), calls=%async_computation | async-start | bytes 262144 | tf_op jit(solution)/shard_map/all_to_all | solution.py:57
  30.8 0.0 reduce-scatter.7.cloned.1.call-start
  30.9 12.3 %all-gather = bf16[8,1,128]{2,1,0:T(2,128)(2,1)S(1)} all-gather(bf16[1,1,128]{2,1,0:T(2,128)(2,1)S(1)} %bitcast.257), channel_id=1, replica_groups=mesh['tower'=4,'rank'=8] {'rank'}, dimensions={0}, use_global_device_ids=true | all-gather | bytes 2304 | tf_op jit(solution)/shard_map/all_gather | solution.py:66
  43.2 0.0 copy-done.4
  43.2 10.9 %all-gather.1 = bf16[8,1,128]{2,1,0:T(2,128)(2,1)S(1)} all-gather(bf16[1,1,128]{2,1,0:T(2,128)(2,1)S(1)} %bitcast.258), channel_id=1, replica_groups=mesh['tower'=4,'rank'=8] {'rank'}, dimensions={0}, use_global_device_ids=true | all-gather | bytes 2304 | tf_op jit(solution)/shard_map/all_gather | solution.py:67
  54.2 0.0 copy-done.1
  54.2 0.6 gather_fusion.1
  54.8 0.0 all-to-all-done
  54.8 0.6 gather_fusion
  55.3 0.1 broadcast_select_fusion.1
  55.4 0.1 copy.35
  55.6 0.1 copy.34
  55.7 0.3 fusion.30
  56.0 0.3 fusion.31
  56.4 0.3 fusion.34
  56.7 0.0 copy-start.2
  56.7 0.5 multiply_reduce_fusion
  57.2 0.3 fusion.32
  57.5 0.5 multiply_reduce_fusion.1
  58.0 0.1 fusion.66
  58.1 8.6 %all_gather.15 = bf16[512,128]{1,0:T(8,128)(2,1)S(1)} all-gather(bf16[128,128]{1,0:T(8,128)(2,1)S(1)} %get-tuple-element.11), channel_id=1, replica_groups=mesh['tower'=4,'rank'=8] {'tower'}, dimensions={0}, use_global_device_ids=true | all-gather | bytes 163840 | tf_op jit(solution)/shard_map/all_gather | solution.py:79
  66.7 0.1 copy.21
  66.9 8.4 %all_gather.19 = bf16[512,128]{1,0:T(8,128)(2,1)S(1)} all-gather(bf16[128,128]{1,0:T(8,128)(2,1)S(1)} %get-tuple-element.12), channel_id=1, replica_groups=mesh['tower'=4,'rank'=8] {'tower'}, dimensions={0}, use_global_device_ids=true | all-gather | bytes 163840 | tf_op jit(solution)/shard_map/all_gather | solution.py:79
  75.3 0.1 copy.27
  75.4 0.3 fusion.12
  75.7 0.3 fusion.7
  76.0 0.7 fusion.28
  76.7 0.7 fusion.29
  77.4 0.0 all-gather.4.cloned.1.call-done
  77.4 1.9 %fusion.5 = f32[128]{0:T(128)S(1)} fusion(bf16[1024,512]{1,0:T(8,128)(2,1)} %all-gather.4.cloned.1.call-done, f32[1024]{0:T(1024)S(1)} %bitcast.244, f32[1024]{0:T(1024)S(1)} %bitcast.242, bf16[16,8,4,128]{3,2,1,0:T(4,128)(2,1)S(1)} %bitcast.239), kind=kOutput, calls=%fused_computation.9 | convolution fusion | flops 134741888 | bytes 1188352 | tf_op jit(solution)/shard_map/dot_general | solution.py:35
  79.3 0.7 copy.36
  80.0 0.0 reduce-scatter.7.cloned.1.call-update
  80.1 0.0 reduce-scatter.9.cloned.1.call-start
  80.1 0.6 fusion.4
  80.7 0.7 copy.38
  81.4 0.0 reduce-scatter.9.cloned.1.call-update
  81.5 20.1 %reduce-scatter.7.cloned.1.call-done = f32[32,1]{1,0:T(8,128)} async-done(((f32[128,1]{1,0:T(8,128)}), f32[32,1]{1,0:T(8,128)}) %reduce-scatter.7.cloned.1.call-update) | async-done | bytes 144
  101.5 0.8 copy.37
  102.3 26.1 %reduce-scatter.9.cloned.1.call-done = f32[32,1]{1,0:T(8,128)} async-done(((f32[128,1]{1,0:T(8,128)}), f32[32,1]{1,0:T(8,128)}) %reduce-scatter.9.cloned.1.call-update) | async-done | bytes 144
  128.4 0.8 copy.39
  129.2 0.6 pad_maximum_fusion
  (16 shorter events, 0.0 us)
Async XLA Ops:
  6.5 50.1 %copy-start = (bf16[1,128,512]{2,1,0:T(8,128)(2,1)S(1)}, bf16[1,128,512]{2,1,0:T(8,128)(2,1)}, u32[]{:S(2)}) copy-start(bf16[1,128,512]{2,1,0:T(8,128)(2,1)} %param.15) | copy-start | bytes 393220
  6.5 24.4 %copy-start.3 = (bf16[128]{0:T(256)(128)(2,1)S(1)}, bf16[128]{0:T(256)(128)(2,1)}, u32[]{:S(2)}) copy-start(bf16[128]{0:T(256)(128)(2,1)} %param.18) | copy-start | bytes 772
  6.5 36.7 %copy-start.4 = (bf16[128]{0:T(256)(128)(2,1)S(1)}, bf16[128]{0:T(256)(128)(2,1)}, u32[]{:S(2)}) copy-start(bf16[128]{0:T(256)(128)(2,1)} %param.19) | copy-start | bytes 772
  6.5 47.6 %copy-start.1 = (f32[1,3,512]{2,0,1:T(1,128)S(1)}, f32[1,3,512]{2,0,1:T(1,128)}, u32[]{:S(2)}) copy-start(f32[1,3,512]{2,0,1:T(1,128)} %param.14) | copy-start | bytes 18436
  6.5 49.1 %copy-start.5 = (bf16[1,3,512,512]{3,2,1,0:T(8,128)(2,1)S(1)}, bf16[1,3,512,512]{3,2,1,0:T(8,128)(2,1)}, u32[]{:S(2)}) copy-start(bf16[1,3,512,512]{3,2,1,0:T(8,128)(2,1)} %param.13) | copy-start | bytes 4718596
  12.5 13.3 %all-to-all-start.1 = ((bf16[8,64,128]{2,1,0:T(8,128)(2,1)}), bf16[8,64,128]{2,1,0:T(8,128)(2,1)S(1)}, u32[]{:S(2)}, u32[]{:S(2)}) async-start(bf16[8,64,128]{2,1,0:T(8,128)(2,1)} %constant_dynamic-update-slice_fusion.8), calls=%async_computation.1 | async-start | bytes 262144 | tf_op jit(solution)/shard_map/all_to_all | solution.py:57
  18.9 58.6 %all-gather.4.cloned.1.call-start = ((), (), s32[]{:S(2)}) async-start(), calls=%async_computation.4 | async-start | bytes 1179648 | tf_op jit(solution)/shard_map/all_gather | solution.py:65
  25.8 29.0 %all-to-all-start = ((bf16[8,64,128]{2,1,0:T(8,128)(2,1)}), bf16[8,64,128]{2,1,0:T(8,128)(2,1)S(1)}, u32[]{:S(2)}, u32[]{:S(2)}) async-start(bf16[8,64,128]{2,1,0:T(8,128)(2,1)} %constant_dynamic-update-slice_fusion), calls=%async_computation | async-start | bytes 262144 | tf_op jit(solution)/shard_map/all_to_all | solution.py:57
  30.8 70.7 %reduce-scatter.7.cloned.1.call-start = ((), (), s32[]{:S(2)}) async-start(), calls=%async_computation.5 | async-start | bytes 81920
  56.7 1.3 copy-start.2
  77.4 2.7 %copy-start.6 = (bf16[1024,512]{1,0:T(8,128)(2,1)S(1)}, bf16[1024,512]{1,0:T(8,128)(2,1)}, u32[]{:S(2)}) copy-start(bf16[1024,512]{1,0:T(8,128)(2,1)} %all-gather.4.cloned.1.call-done) | copy-start | bytes 3145732
  80.1 48.3 %reduce-scatter.9.cloned.1.call-start = ((), (), s32[]{:S(2)}) async-start(), calls=%async_computation.6 | async-start | bytes 81920
Sparse Core Ops, SparseCore 0:
  21.3 25.8 all-gather.3
  80.2 21.3 reduce-scatter.6
  104.3 24.0 reduce-scatter.8
